TPU v7x, 256 devices: a whole 4x4x8 slice. The times are simulated.
256 devices in a mesh: seq: 64 (over z_lo, x, y), batch: 4 (over z_hi, core).
Axes of the slice: x: 4, y: 4, z: 8 (z_hi: 2, z_lo: 4; z = z_hi * 4 + z_lo), core: 2. Of those that a mesh axis runs over, the one named last changes fastest.
Arguments:
- inputs: bfloat16 [4, 16384, 2048], P('batch', 'seq'), may hold values from -106.50967 to 106.50967
- output_grad: bfloat16 [4, 16384, 2048], P('batch', 'seq'), may hold values from -6 to 6
- norm_gain: float32 [2048], replicated, may hold values from 0.1 to 1.9
- gate_bias: float32 [2048], P('seq'), as said below
- state_in: float32 [4, 2048], P('batch', 'seq'), may hold values from -6 to 6
- w_gate: bfloat16 [2048, 2048], P('seq'), may hold values from -0.44194174 to 0.44194174
- w_cand: bfloat16 [2048, 2048], P('seq'), may hold values from -0.125 to 0.125
- w_out: bfloat16 [2048, 2048], P('seq'), may hold values from -0.125 to 0.125
Outputs:
- layer_out: bfloat16 [4, 16384, 2048], P('batch', 'seq')
- input_grad: bfloat16 [4, 16384, 2048], P('batch', 'seq')
- state_grad: float32 [4, 2048], P('batch', 'seq')
- bias_grad: float32 [2048], P('seq')
Inputs may be any that keep to these rules, and one draw needn't show every extreme that they name: `gate_bias`: every value is at least -ln(16384) - 1.5.
All inputs are finite; a program needn't handle non-finite values.
Results may differ from a plain program's by a relative error of at most 0.013.
Values may be sent and summed in bfloat16 or wider, within the bound.
A program may use at most 128 MiB of HBM per device.

v0:
```python
import jax
import jax.numpy as jnp
from jax import lax
from jax.sharding import PartitionSpec as P

EPSILON = 1e-06


def shifted(values, axis, offset, fill, reverse):
    length = values.shape[axis]
    pad_shape = list(values.shape)
    pad_shape[axis] = offset
    padding = jnp.full(tuple(pad_shape), fill, values.dtype)
    if reverse:
        kept = lax.slice_in_dim(values, offset, length, 1, axis)
        return jnp.concatenate([kept, padding], axis=axis)
    kept = lax.slice_in_dim(values, 0, length - offset, 1, axis)
    return jnp.concatenate([padding, kept], axis=axis)


def shift_scan(keep, drive, axis, reverse):
    length = keep.shape[axis]
    offset = 1
    while offset < length:
        keep_far = shifted(keep, axis, offset, 1.0, reverse)
        drive_far = shifted(drive, axis, offset, 0.0, reverse)
        drive = keep * drive_far + drive
        keep = keep * keep_far
        offset = offset * 2
    return (keep, drive)


def on_device(inputs, output_grad, norm_gain, gate_bias, state_in, w_gate, w_cand, w_out):
    token_rows = inputs[0]
    grad_rows = output_grad[0]
    gate_full, cand_full, out_full = (
        lax.all_gather(w_gate, "seq", axis=0, tiled=True),
        lax.all_gather(w_cand, "seq", axis=0, tiled=True),
        lax.all_gather(w_out, "seq", axis=0, tiled=True),
    )
    residual = token_rows.astype(jnp.float32)
    mean_square = jnp.mean(residual * residual, axis=-1, keepdims=True)
    inverse_rms = lax.rsqrt(mean_square + EPSILON)
    unit_rows = residual * inverse_rms
    normed = (unit_rows * norm_gain).astype(jnp.bfloat16)
    hidden_dim = 0
    contract_model = (((0,), (1,)), ((), ()))
    gate_pre = lax.dot_general(
        gate_full, normed, contract_model, preferred_element_type=jnp.float32
    ).astype(jnp.bfloat16)
    cand_pre = lax.dot_general(
        cand_full, normed, contract_model, preferred_element_type=jnp.float32
    ).astype(jnp.bfloat16)
    back_grads = lax.dot_general(
        out_full, grad_rows, (((1,), (1,)), ((), ())), preferred_element_type=jnp.float32
    ).astype(jnp.bfloat16)
    gate_slab, cand_slab = (
        lax.all_to_all(gate_pre, "seq", split_axis=0, concat_axis=1, tiled=True),
        lax.all_to_all(cand_pre, "seq", split_axis=0, concat_axis=1, tiled=True),
    )
    gate_input = gate_slab.astype(jnp.float32) + gate_bias[:, None]
    update = jax.nn.sigmoid(gate_input)
    retain = jax.nn.sigmoid(-gate_input)
    candidate = cand_slab.astype(jnp.float32)
    initial = state_in[0]
    drive_term = (update * candidate).at[:, 0].add(retain[:, 0] * initial)
    reached, states = shift_scan(retain, drive_term, 1, False)
    state_tok = lax.all_to_all(
        states.astype(jnp.bfloat16), "seq", split_axis=1, concat_axis=0, tiled=True
    )
    back_slab = lax.all_to_all(back_grads, "seq", split_axis=0, concat_axis=1, tiled=True)
    next_retain = jnp.concatenate(
        [retain[:, 1:], jnp.zeros((retain.shape[0], 1), jnp.float32)], axis=1
    )
    tail_keep, carried = shift_scan(next_retain, back_slab.astype(jnp.float32), 1, True)
    state_grad = retain[:, 0] * carried[:, 0]
    earlier_states = jnp.concatenate([initial[:, None], states[:, :-1]], axis=1)
    gate_grad = carried * (candidate - earlier_states) * update * retain
    cand_grad = carried * update
    bias_part = jnp.sum(gate_grad, axis=1)
    gate_tok, cand_tok = (
        lax.all_to_all(
            gate_grad.astype(jnp.bfloat16), "seq", split_axis=1, concat_axis=0, tiled=True
        ),
        lax.all_to_all(
            cand_grad.astype(jnp.bfloat16), "seq", split_axis=1, concat_axis=0, tiled=True
        ),
    )
    contract_hidden = (((hidden_dim,), (0,)), ((), ()))
    layer_rows = (
        residual
        + lax.dot_general(state_tok, out_full, contract_hidden, preferred_element_type=jnp.float32)
    ).astype(jnp.bfloat16)
    contract_back = (((hidden_dim,), (1,)), ((), ()))
    normed_grad = lax.dot_general(
        gate_tok, gate_full, contract_back, preferred_element_type=jnp.float32
    )
    normed_grad = normed_grad + lax.dot_general(
        cand_tok, cand_full, contract_back, preferred_element_type=jnp.float32
    )
    unit_grad = normed_grad * norm_gain
    input_rows = inverse_rms * (
        unit_grad - unit_rows * jnp.mean(unit_grad * unit_rows, axis=-1, keepdims=True)
    )
    token_grad = (grad_rows.astype(jnp.float32) + input_rows).astype(jnp.bfloat16)
    bias_grad = lax.psum(bias_part, "batch")
    return (layer_rows[None], token_grad[None], state_grad[None], bias_grad)


def solution(mesh):
    return jax.shard_map(
        on_device,
        mesh=mesh,
        in_specs=(
            P("batch", "seq", None),
            P("batch", "seq", None),
            P(),
            P("seq"),
            P("batch", "seq"),
            P("seq", None),
            P("seq", None),
            P("seq", None),
        ),
        out_specs=(P("batch", "seq", None), P("batch", "seq", None), P("batch", "seq"), P("seq")),
        check_vma=False,
    )
```

profile of v0, /device:TPU:8, one launch (start us, length us, event | category | flops | bytes accessed | tf_op | source)
XLA Modules:
  0.0 1306.1 jit_solution(2977227251477616313)
XLA Ops:
  9.4 1.5 fusion.14
  10.9 361.7 %all-gather.6.cloned.1.call-done = bf16[2048,2048]{1,0:T(8,128)(2,1)} async-done(((bf16[32,2048]{1,0:T(8,128)(2,1)}), bf16[2048,2048]{1,0:T(8,128)(2,1)}) %all-gather.6.cloned.1.call-update) | async-done | bytes 8388624 | tf_op jit(solution)/shard_map/all_gather | solution.py:38
  372.6 6.1 fusion.6
  378.7 1.3 copy.33
  380.0 10.6 all-to-all-start.1
  390.6 343.9 %all-gather.4.cloned.1.call-done = bf16[2048,2048]{1,0:T(8,128)(2,1)} async-done(((bf16[32,2048]{1,0:T(8,128)(2,1)}), bf16[2048,2048]{1,0:T(8,128)(2,1)}) %all-gather.4.cloned.1.call-update) | async-done | bytes 8388624 | tf_op jit(solution)/shard_map/all_gather | solution.py:37
  734.5 6.7 fusion.5
  741.2 2.3 copy.31
  743.6 9.9 all-to-all-start
  753.5 340.4 %all-gather.8.cloned.1.call-done = bf16[2048,2048]{1,0:T(8,128)(2,1)} async-done(((bf16[32,2048]{1,0:T(8,128)(2,1)}), bf16[2048,2048]{1,0:T(8,128)(2,1)}) %all-gather.8.cloned.1.call-update) | async-done | bytes 8388624 | tf_op jit(solution)/shard_map/all_gather | solution.py:39
  1093.9 6.7 convolution_convert_fusion
  1100.6 11.7 all-to-all-start.3
  1113.3 1.6 copy.45
  1115.2 1.5 copy.44
  1116.7 13.5 %all-to-all-done.3 = bf16[64,32,256]{2,1,0:T(8,128)(2,1)} async-done(((bf16[64,32,256]{2,1,0:T(8,128)(2,1)}), bf16[64,32,256]{2,1,0:T(8,128)(2,1)}, u32[]{:S(2)}, u32[]{:S(2)}) %all-to-all-start.3) | async-done | bytes 1048608 | tf_op jit(solution)/shard_map/all_to_all | solution.py:71
  1130.2 1.5 convert_bitcast_fusion
  1131.9 2.0 slice.294
  1135.6 1.2 add_divide_fusion.1
  1136.8 2.6 fusion.27
  1140.0 1.3 scatter-add.4
  1141.4 4.3 multiply_add_fusion.27
  1148.3 2.5 slice_multiply_fusion
  1151.8 2.1 slice.296
  1153.9 10.3 multiply_add_fusion.11
  1164.2 4.6 multiply_add_fusion.25
  1168.8 1.1 multiply_add_fusion.24
  1170.0 1.1 multiply_add_fusion.23
  1171.1 1.1 multiply_add_fusion.22
  1172.3 1.1 multiply_add_fusion.21
  1173.6 9.4 multiply_add_fusion.20
  1186.5 1.5 copy-done.10
  1201.0 1.2 copy-done.3
  1202.8 2.9 fusion.24
  1205.7 1.1 copy.51
  1206.8 6.2 all-to-all-start.4
  1213.0 2.8 multiply_convert_fusion
  1215.9 1.1 copy.50
  1217.0 14.3 %all-to-all-done.4 = bf16[32,64,256]{2,0,1:T(8,128)(2,1)} async-done(((bf16[32,64,256]{2,0,1:T(8,128)(2,1)}), bf16[32,64,256]{2,0,1:T(8,128)(2,1)}, u32[]{:S(2)}, u32[]{:S(2)}) %all-to-all-start.4) | async-done | bytes 1048608 | tf_op jit(solution)/shard_map/all_to_all | solution.py:82
  1231.2 6.2 all-to-all-start.5
  1237.5 1.1 copy.52
  1238.6 16.1 %psum.7 = f32[32]{0:T(128)} all-reduce(f32[32]{0:T(128)S(1)} %get-tuple-element.16), channel_id=1, replica_groups=mesh['seq'=64,'batch'=4] {'batch'}, use_global_device_ids=true, to_apply=%region_4.0 | all-reduce | flops 32 | bytes 256 | tf_op jit(solution)/shard_map/psum | solution.py:106
  1254.7 1.3 fusion.22
  1256.1 11.1 all-to-all-start.2
  1267.2 6.2 fusion.28
  1273.4 6.5 fusion.9
  1280.0 1.6 fusion.18
  1281.6 10.9 all-to-all-done.2
  1292.5 6.7 fusion.7
  (120 shorter events, 26.6 us)
Async XLA Ops:
  7.2 365.4 %all-gather.6.cloned.1.call-start = ((), (), s32[]{:S(2)}) async-start(), calls=%async_computation.7 | async-start | bytes 8519680 | tf_op jit(solution)/shard_map/all_gather | solution.py:38
  7.9 726.6 %all-gather.4.cloned.1.call-start = ((), (), s32[]{:S(2)}) async-start(), calls=%async_computation.6 | async-start | bytes 8519680 | tf_op jit(solution)/shard_map/all_gather | solution.py:37
  8.6 1085.2 %all-gather.8.cloned.1.call-start = ((), (), s32[]{:S(2)}) async-start(), calls=%async_computation.8 | async-start | bytes 8519680 | tf_op jit(solution)/shard_map/all_gather | solution.py:39
  10.9 723.6 %copy-start.20 = (f32[256]{0:T(256)}, f32[256]{0:T(256)S(1)}, u32[]{:S(2)}) copy-start(f32[256]{0:T(256)S(1)} %add_rsqrt_fusion) | copy-start | bytes 3076
  378.7 355.8 %copy-start.12 = (bf16[1,256,2048]{2,1,0:T(8,128)(2,1)S(1)}, bf16[1,256,2048]{2,1,0:T(8,128)(2,1)}, u32[]{:S(2)}) copy-start(bf16[1,256,2048]{2,1,0:T(8,128)(2,1)} %param.10) | copy-start | bytes 3145732
  378.7 355.8 %copy-start.23 = (f32[2048]{0:T(1024)S(1)}, f32[2048]{0:T(1024)}, u32[]{:S(2)}) copy-start(f32[2048]{0:T(1024)} %param.12) | copy-start | bytes 24580
  380.0 363.5 %all-to-all-start.1 = ((bf16[64,32,256]{2,1,0:T(8,128)(2,1)}), bf16[64,32,256]{2,1,0:T(8,128)(2,1)S(1)}, u32[]{:S(2)}, u32[]{:S(2)}) async-start(bf16[64,32,256]{2,1,0:T(8,128)(2,1)} %bitcast.6), calls=%async_computation.1 | async-start | bytes 2097152 | tf_op jit(solution)/shard_map/all_to_all | solution.py:59
  741.2 352.6 %copy-start.17 = (bf16[1,256,2048]{2,1,0:T(8,128)(2,1)S(1)}, bf16[1,256,2048]{2,1,0:T(8,128)(2,1)}, u32[]{:S(2)}) copy-start(bf16[1,256,2048]{2,1,0:T(8,128)(2,1)} %param.11) | copy-start | bytes 3145732
  743.6 357.0 %all-to-all-start = ((bf16[64,32,256]{2,1,0:T(8,128)(2,1)}), bf16[64,32,256]{2,1,0:T(8,128)(2,1)S(1)}, u32[]{:S(2)}, u32[]{:S(2)}) async-start(bf16[64,32,256]{2,1,0:T(8,128)(2,1)} %bitcast.3), calls=%async_computation | async-start | bytes 2097152 | tf_op jit(solution)/shard_map/all_to_all | solution.py:58
  1100.6 11.7 copy-start.22
  1100.6 11.8 copy-start.15
  1100.6 29.6 %all-to-all-start.3 = ((bf16[64,32,256]{2,1,0:T(8,128)(2,1)}), bf16[64,32,256]{2,1,0:T(8,128)(2,1)}, u32[]{:S(2)}, u32[]{:S(2)}) async-start(bf16[64,32,256]{2,1,0:T(8,128)(2,1)} %bitcast.110), calls=%async_computation.3 | async-start | bytes 2097152 | tf_op jit(solution)/shard_map/all_to_all | solution.py:71
  1113.3 1.6 copy-start.16
  1131.8 2.1 copy-start.5
  1131.9 3.1 copy-start.2
  1131.9 3.7 copy-start.8
  1131.9 3.7 copy-start.19
  1136.8 2.6 copy-start.4
  1141.4 4.3 copy-start
  1145.7 1.6 copy-start.6
  1145.7 2.2 copy-start.14
  1147.9 3.5 copy-start.1
  1151.8 2.1 copy-start.7
  1186.4 1.6 copy-start.10
  1188.0 1.6 copy-start.11
  1200.6 1.6 copy-start.3
  1200.6 2.2 copy-start.9
  1206.8 24.5 %all-to-all-start.4 = ((bf16[32,64,256]{2,0,1:T(8,128)(2,1)}), bf16[32,64,256]{2,0,1:T(8,128)(2,1)}, u32[]{:S(2)}, u32[]{:S(2)}) async-start(bf16[32,64,256]{2,0,1:T(8,128)(2,1)} %bitcast.107), calls=%async_computation.4 | async-start | bytes 2097152 | tf_op jit(solution)/shard_map/all_to_all | solution.py:82
  1231.2 24.8 %all-to-all-start.5 = ((bf16[32,64,256]{2,0,1:T(8,128)(2,1)}), bf16[32,64,256]{2,0,1:T(8,128)(2,1)}, u32[]{:S(2)}, u32[]{:S(2)}) async-start(bf16[32,64,256]{2,0,1:T(8,128)(2,1)} %bitcast.106), calls=%async_computation.5 | async-start | bytes 2097152 | tf_op jit(solution)/shard_map/all_to_all | solution.py:85
  1256.1 36.4 %all-to-all-start.2 = ((bf16[32,64,256]{2,0,1:T(8,128)(2,1)}), bf16[32,64,256]{2,0,1:T(8,128)(2,1)S(1)}, u32[]{:S(2)}, u32[]{:S(2)}) async-start(bf16[32,64,256]{2,0,1:T(8,128)(2,1)} %bitcast.105), calls=%async_computation.2 | async-start | bytes 2097152 | tf_op jit(solution)/shard_map/all_to_all | solution.py:68
  1267.2 6.2 copy-start.13
  1267.2 6.2 copy-start.21
  1267.2 6.2 copy-start.24
  1273.4 6.5 copy-start.18
Sparse Core Ops, SparseCore 0:
  9.8 362.7 all-gather.5
  374.4 360.0 all-gather.3
  736.3 357.5 all-gather.7
where the time goes:
time: 1310 us
  waiting for transfers between devices  1090 us (83%)
  other arithmetic  57.8 us (4%)
  starting transfers between devices  55.8 us (4%)
  matrix products  39 us (3%)
  local copies, waits for them, and re-layouts  36 us (3%)
  blocking collectives  16.1 us (1%)
  between operations  14.9 us (1%)
    all_gather x1, waiting for transfers between devices, on_device(): lax.all_gather(w_cand, 'seq', axis=0, tiled=True)  362 us
    all_gather x1, waiting for transfers between devices, on_device(): lax.all_gather(w_gate, 'seq', axis=0, tiled=True)  344 us
    all_gather x1, waiting for transfers between devices, on_device(): lax.all_gather(w_out, 'seq', axis=0, tiled=True)  340 us
    add x25, other arithmetic, shift_scan(): drive = keep * drive_far + drive  40.3 us
  transfers between devices with their start and end apart: 9, of which 6 were waited for; matrix products, arithmetic and copies ran while one was open for 4% of the time, Pallas kernels for 0%

commit v1 on v0

--- a/solution.py
+++ b/solution.py
@@ -36,7 +36,9 @@
     gate_full, cand_full, out_full = (
         lax.all_gather(w_gate, "seq", axis=0, tiled=True),
         lax.all_gather(w_cand, "seq", axis=0, tiled=True),
-        lax.all_gather(w_out, "seq", axis=0, tiled=True),
+        jnp.concatenate(
+            lax.all_to_all(jnp.stack([w_out] * lax.axis_size("seq")), "seq", 0, 0), axis=0
+        ),
     )
     residual = token_rows.astype(jnp.float32)
     mean_square = jnp.mean(residual * residual, axis=-1, keepdims=True)

time: 1310 us -> 1040 us (0.79)
  waiting for transfers between devices: 1090 us -> 790 us
  starting transfers between devices: 55.8 us -> 75.7 us
    all_gather x1 -> x0, waiting for transfers between devices: 340 us -> none  [on_device(): lax.all_gather(w_out, 'seq', axis=0, tiled=True)]
    all_to_all x0 -> x1, waiting for transfers between devices: none -> 226 us  [on_device(): lax.all_to_all(jnp.stack([w_out] * lax.axis_size('seq')), 'seq', 0, 0)]
    all_gather x1, waiting for transfers between devices: 344 us -> 178 us  [on_device(): lax.all_gather(w_gate, 'seq', axis=0, tiled=True)]
    all_gather x1, waiting for transfers between devices: 362 us -> 347 us  [on_device(): lax.all_gather(w_cand, 'seq', axis=0, tiled=True)]
    all_to_all x1, waiting for transfers between devices: 13.5 us -> 0.01 us  [on_device(): lax.all_to_all(back_grads, 'seq', split_axis=0, concat_axis=1, tiled=True)]
  transfers between devices with their start and end apart: 9 -> 9, of which waited for: 6 -> 7; matrix products, arithmetic and copies ran while one was open for 4% -> 5% of each run, Pallas kernels for 0% -> 0%
where the time goes in v1:
time: 1040 us; the launch traced here: 1030 us
  waiting for transfers between devices  790 us (76%)
  starting transfers between devices  75.7 us (7%)
  other arithmetic  47.8 us (5%)
  matrix products  47.2 us (5%)
  local copies, waits for them, and re-layouts  40.5 us (4%)
  blocking collectives  15.8 us (2%)
  between operations  15.2 us (1%)
    all_gather x1, waiting for transfers between devices, on_device(): lax.all_gather(w_cand, 'seq', axis=0, tiled=True)  347 us
    all_to_all x1, waiting for transfers between devices, on_device(): lax.all_to_all(jnp.stack([w_out] * lax.axis_size('seq')), 'seq', 0, 0)  226 us
    all_gather x1, waiting for transfers between devices, on_device(): lax.all_gather(w_gate, 'seq', axis=0, tiled=True)  178 us
    add x25, other arithmetic, shift_scan(): drive = keep * drive_far + drive  31.4 us
  transfers between devices with their start and end apart: 9, of which 7 were waited for; matrix products, arithmetic and copies ran while one was open for 5% of the time, Pallas kernels for 0%

profile of v1, /device:TPU:8, one launch (start us, length us, event | category | flops | bytes accessed | tf_op | source)
XLA Modules:
  0.0 1032.5 jit_solution(16877041166737827157)
XLA Ops:
  7.9 5.2 stack.2
  13.1 12.3 %all-to-all-start.3 = ((bf16[64,32,2048]{2,1,0:T(8,128)(2,1)}), bf16[64,32,2048]{2,1,0:T(8,128)(2,1)}, u32[]{:S(2)}, u32[]{:S(2)}) async-start(bf16[64,32,2048]{2,1,0:T(8,128)(2,1)} %stack.2), calls=%async_computation.3 | async-start | bytes 16777216 | tf_op jit(solution)/shard_map/all_to_all | solution.py:40
  26.2 226.5 %all-to-all-done.3 = bf16[64,32,2048]{2,1,0:T(8,128)(2,1)} async-done(((bf16[64,32,2048]{2,1,0:T(8,128)(2,1)}), bf16[64,32,2048]{2,1,0:T(8,128)(2,1)}, u32[]{:S(2)}, u32[]{:S(2)}) %all-to-all-start.3) | async-done | bytes 8388640 | tf_op jit(solution)/shard_map/all_to_all | solution.py:40
  252.7 6.8 convolution_convert_fusion
  259.5 19.6 %all-to-all-start.4 = ((bf16[64,32,256]{2,1,0:T(8,128)(2,1)}), bf16[64,32,256]{2,1,0:T(8,128)(2,1)S(1)}, u32[]{:S(2)}, u32[]{:S(2)}) async-start(bf16[64,32,256]{2,1,0:T(8,128)(2,1)} %bitcast.14), calls=%async_computation.4 | async-start | bytes 2097152 | tf_op jit(solution)/shard_map/all_to_all | solution.py:73
  279.4 177.5 %all-gather.3.cloned.1.call-done = bf16[2048,2048]{1,0:T(8,128)(2,1)} async-done(((bf16[32,2048]{1,0:T(8,128)(2,1)}), bf16[2048,2048]{1,0:T(8,128)(2,1)}) %all-gather.3.cloned.1.call-update) | async-done | bytes 8388624 | tf_op jit(solution)/shard_map/all_gather | solution.py:37
  456.9 5.8 fusion.14
  462.7 1.3 copy.43
  464.0 9.9 all-to-all-start
  473.9 347.0 %all-gather.5.cloned.1.call-done = bf16[2048,2048]{1,0:T(8,128)(2,1)} async-done(((bf16[32,2048]{1,0:T(8,128)(2,1)}), bf16[2048,2048]{1,0:T(8,128)(2,1)}) %all-gather.5.cloned.1.call-update) | async-done | bytes 8388624 | tf_op jit(solution)/shard_map/all_gather | solution.py:38
  820.9 6.7 fusion.15
  827.6 2.3 copy.45
  829.9 10.4 %all-to-all-start.1 = ((bf16[64,32,256]{2,1,0:T(8,128)(2,1)}), bf16[64,32,256]{2,1,0:T(8,128)(2,1)}, u32[]{:S(2)}, u32[]{:S(2)}) async-start(bf16[64,32,256]{2,1,0:T(8,128)(2,1)} %bitcast.6), calls=%async_computation.1 | async-start | bytes 2097152 | tf_op jit(solution)/shard_map/all_to_all | solution.py:61
  841.6 2.1 slice.294
  843.9 1.5 copy.58
  845.4 12.9 %all-to-all-done.1 = bf16[64,32,256]{2,1,0:T(8,128)(2,1)} async-done(((bf16[64,32,256]{2,1,0:T(8,128)(2,1)}), bf16[64,32,256]{2,1,0:T(8,128)(2,1)}, u32[]{:S(2)}, u32[]{:S(2)}) %all-to-all-start.1) | async-done | bytes 1048608 | tf_op jit(solution)/shard_map/all_to_all | solution.py:61
  858.3 1.5 convert_bitcast_fusion.1
  860.0 2.1 copy-done.2
  862.1 1.2 add_divide_fusion.1
  863.3 2.0 fusion.40
  865.9 1.7 copy-done.6
  869.3 2.5 slice_multiply_fusion
  872.2 2.1 slice.296
  875.0 1.7 scatter-add.4
  876.7 4.2 multiply_add_fusion.27
  880.9 10.3 multiply_add_fusion.11
  891.1 4.6 multiply_add_fusion.25
  895.7 1.1 multiply_add_fusion.24
  896.9 1.1 multiply_add_fusion.23
  898.0 1.1 multiply_add_fusion.22
  899.2 1.1 multiply_add_fusion.21
  904.9 1.5 copy-done.10
  920.9 2.8 fusion.37
  923.8 1.1 copy.79
  924.9 6.2 all-to-all-start.5
  931.2 2.8 multiply_convert_fusion
  934.0 1.1 copy.78
  935.1 14.3 %all-to-all-done.5 = bf16[32,64,256]{2,0,1:T(8,128)(2,1)} async-done(((bf16[32,64,256]{2,0,1:T(8,128)(2,1)}), bf16[32,64,256]{2,0,1:T(8,128)(2,1)}, u32[]{:S(2)}, u32[]{:S(2)}) %all-to-all-start.5) | async-done | bytes 1048608 | tf_op jit(solution)/shard_map/all_to_all | solution.py:84
  949.4 6.2 all-to-all-start.6
  955.6 1.1 copy.80
  956.7 15.8 %psum.7 = f32[32]{0:T(128)} all-reduce(f32[32]{0:T(128)S(1)} %get-tuple-element.16), channel_id=1, replica_groups=mesh['seq'=64,'batch'=4] {'batch'}, use_global_device_ids=true, to_apply=%region_4.0 | all-reduce | flops 32 | bytes 256 | tf_op jit(solution)/shard_map/psum | solution.py:108
  972.5 1.3 fusion.35
  974.0 10.9 %all-to-all-start.2 = ((bf16[32,64,256]{2,0,1:T(8,128)(2,1)}), bf16[32,64,256]{2,0,1:T(8,128)(2,1)S(1)}, u32[]{:S(2)}, u32[]{:S(2)}) async-start(bf16[32,64,256]{2,0,1:T(8,128)(2,1)} %bitcast.111), calls=%async_computation.2 | async-start | bytes 2097152 | tf_op jit(solution)/shard_map/all_to_all | solution.py:70
  985.0 6.2 fusion.41
  991.2 6.5 fusion.20
  997.7 1.6 fusion.29
  999.3 10.7 %all-to-all-done.2 = bf16[32,64,256]{2,0,1:T(8,128)(2,1)S(1)} async-done(((bf16[32,64,256]{2,0,1:T(8,128)(2,1)}), bf16[32,64,256]{2,0,1:T(8,128)(2,1)S(1)}, u32[]{:S(2)}, u32[]{:S(2)}) %all-to-all-start.2) | async-done | bytes 1048608 | tf_op jit(solution)/shard_map/all_to_all | solution.py:70
  1010.0 15.3 %fusion.16 = bf16[1,256,2048]{2,1,0:T(8,128)(2,1)} fusion(bf16[64,32,2048]{2,1,0:T(8,128)(2,1)} %all-to-all-done.3, bf16[1,256,2048]{2,1,0:T(8,128)(2,1)S(1)} %copy-done.14, bf16[32,64,256]{2,0,1:T(8,128)(2,1)S(1)} %all-to-all-done.2), kind=kOutput, calls=%fused_computation.17 | convolution fusion | flops 2149056512 | bytes 11534336 | tf_op jit(solution)/shard_map/dot_general | solution.py:94
  (116 shorter events, 25.7 us)
Async XLA Ops:
  7.2 449.7 %all-gather.3.cloned.1.call-start = ((), (), s32[]{:S(2)}) async-start(), calls=%async_computation.7 | async-start | bytes 8519680 | tf_op jit(solution)/shard_map/all_gather | solution.py:37
  13.1 239.6 %copy-start.15 = (bf16[1,256,2048]{2,1,0:T(8,128)(2,1)S(1)}, bf16[1,256,2048]{2,1,0:T(8,128)(2,1)}, u32[]{:S(2)}) copy-start(bf16[1,256,2048]{2,1,0:T(8,128)(2,1)} %param.11) | copy-start | bytes 3145732
  13.1 239.6 %all-to-all-start.3 = ((bf16[64,32,2048]{2,1,0:T(8,128)(2,1)}), bf16[64,32,2048]{2,1,0:T(8,128)(2,1)}, u32[]{:S(2)}, u32[]{:S(2)}) async-start(bf16[64,32,2048]{2,1,0:T(8,128)(2,1)} %stack.2), calls=%async_computation.3 | async-start | bytes 16777216 | tf_op jit(solution)/shard_map/all_to_all | solution.py:40
  25.5 795.4 %all-gather.5.cloned.1.call-start = ((), (), s32[]{:S(2)}) async-start(), calls=%async_computation.8 | async-start | bytes 8519680 | tf_op jit(solution)/shard_map/all_gather | solution.py:38
  259.5 19.6 %copy-start.13 = (bf16[1,256,2048]{2,1,0:T(8,128)(2,1)S(1)}, bf16[1,256,2048]{2,1,0:T(8,128)(2,1)}, u32[]{:S(2)}) copy-start(bf16[1,256,2048]{2,1,0:T(8,128)(2,1)} %param.10) | copy-start | bytes 3145732
  259.5 197.4 %copy-start.21 = (f32[2048]{0:T(1024)S(1)}, f32[2048]{0:T(1024)}, u32[]{:S(2)}) copy-start(f32[2048]{0:T(1024)} %param.12) | copy-start | bytes 24580
  259.5 204.5 %all-to-all-start.4 = ((bf16[64,32,256]{2,1,0:T(8,128)(2,1)}), bf16[64,32,256]{2,1,0:T(8,128)(2,1)S(1)}, u32[]{:S(2)}, u32[]{:S(2)}) async-start(bf16[64,32,256]{2,1,0:T(8,128)(2,1)} %bitcast.14), calls=%async_computation.4 | async-start | bytes 2097152 | tf_op jit(solution)/shard_map/all_to_all | solution.py:73
  279.4 541.5 %copy-start.18 = (f32[256]{0:T(256)}, f32[256]{0:T(256)S(1)}, u32[]{:S(2)}) copy-start(f32[256]{0:T(256)S(1)} %add_rsqrt_fusion) | copy-start | bytes 3076
  464.0 365.9 %all-to-all-start = ((bf16[64,32,256]{2,1,0:T(8,128)(2,1)}), bf16[64,32,256]{2,1,0:T(8,128)(2,1)S(1)}, u32[]{:S(2)}, u32[]{:S(2)}) async-start(bf16[64,32,256]{2,1,0:T(8,128)(2,1)} %bitcast.113), calls=%async_computation | async-start | bytes 2097152 | tf_op jit(solution)/shard_map/all_to_all | solution.py:60
  827.6 12.8 %copy-start.20 = (f32[1,32]{1,0:T(1,128)S(1)}, f32[1,32]{1,0:T(1,128)}, u32[]{:S(2)}) copy-start(f32[1,32]{1,0:T(1,128)} %param.14) | copy-start | bytes 388
  829.9 28.4 %all-to-all-start.1 = ((bf16[64,32,256]{2,1,0:T(8,128)(2,1)}), bf16[64,32,256]{2,1,0:T(8,128)(2,1)}, u32[]{:S(2)}, u32[]{:S(2)}) async-start(bf16[64,32,256]{2,1,0:T(8,128)(2,1)} %bitcast.6), calls=%async_computation.1 | async-start | bytes 2097152 | tf_op jit(solution)/shard_map/all_to_all | solution.py:61
  841.6 2.1 copy-start.5
  859.8 2.4 copy-start.2
  859.8 2.3 copy-start.17
  860.0 3.3 copy-start.8
  863.3 11.0 %copy-start.4 = (f32[32,16384]{1,0:T(8,128)}, f32[32,16384]{1,0:T(8,128)S(1)}, u32[]{:S(2)}) copy-start(f32[32,16384]{1,0:T(8,128)S(1)} %get-tuple-element.68) | copy-start | bytes 6291460
  865.3 6.5 copy-start
  865.3 2.3 copy-start.6
  865.3 3.0 copy-start.12
  868.3 3.5 copy-start.1
  872.2 2.1 copy-start.7
  904.8 1.6 copy-start.10
  906.4 1.6 copy-start.11
  918.7 1.6 copy-start.3
  918.7 2.2 copy-start.9
  924.9 24.5 %all-to-all-start.5 = ((bf16[32,64,256]{2,0,1:T(8,128)(2,1)}), bf16[32,64,256]{2,0,1:T(8,128)(2,1)}, u32[]{:S(2)}, u32[]{:S(2)}) async-start(bf16[32,64,256]{2,0,1:T(8,128)(2,1)} %bitcast.114), calls=%async_computation.5 | async-start | bytes 2097152 | tf_op jit(solution)/shard_map/all_to_all | solution.py:84
  949.4 24.7 %all-to-all-start.6 = ((bf16[32,64,256]{2,0,1:T(8,128)(2,1)}), bf16[32,64,256]{2,0,1:T(8,128)(2,1)}, u32[]{:S(2)}, u32[]{:S(2)}) async-start(bf16[32,64,256]{2,0,1:T(8,128)(2,1)} %bitcast.112), calls=%async_computation.6 | async-start | bytes 2097152 | tf_op jit(solution)/shard_map/all_to_all | solution.py:87
  974.0 36.0 %all-to-all-start.2 = ((bf16[32,64,256]{2,0,1:T(8,128)(2,1)}), bf16[32,64,256]{2,0,1:T(8,128)(2,1)S(1)}, u32[]{:S(2)}, u32[]{:S(2)}) async-start(bf16[32,64,256]{2,0,1:T(8,128)(2,1)} %bitcast.111), calls=%async_computation.2 | async-start | bytes 2097152 | tf_op jit(solution)/shard_map/all_to_all | solution.py:70
  985.0 6.2 copy-start.14
  985.0 6.2 copy-start.19
  985.0 6.2 copy-start.22
  991.2 6.5 copy-start.16
Sparse Core Ops, SparseCore 0:
  9.8 447.1 all-gather.2
  458.7 362.1 all-gather.4
